TPU v7x, 256 devices: a whole 4x4x8 slice. The times are simulated.
256 devices in a mesh: head: 4 (over x_hi, core), vis: 32 (over y, z), sec: 2 (over x_lo).
Axes of the slice: x: 4 (x_hi: 2, x_lo: 2; x = x_hi * 2 + x_lo), y: 4, z: 8, core: 2. Of those that a mesh axis runs over, the one named last changes fastest.
Arguments:
- text_states: bfloat16 [256, 8192], P(None, 'vis'), may hold values from -6 to 6
- w_query: bfloat16 [8192, 8192], P('vis', ('head', 'sec')), may hold values from -0.0625 to 0.0625
- w_out: bfloat16 [8192, 8192], P(('head', 'sec'), 'vis'), may hold values from -0.25 to 0.25
- visual_keys: bfloat16 [262144, 1024], P('vis', ('head', 'sec')), may hold values from -120 to 120
- visual_values: bfloat16 [262144, 1024], P('vis', ('head', 'sec')), may hold values from -6 to 6
- block_list: int32 [2, 32, 32], P(None, 'vis'), may hold values from -1 to 63, as said below
Outputs:
- projected: bfloat16 [256, 8192], P(('head', 'sec'), 'vis')
Inputs may be any that keep to these rules, and one draw needn't show every extreme that they name: `block_list`: for each query block and shard, the entries that are not -1 are distinct and come first; each query block selects exactly 512 key blocks in all (a quarter), between 0 and 32 from one shard, and exactly 32 from some shard.
All inputs are finite; a program needn't handle non-finite values.
Results may differ from a plain program's by a relative error of at most 0.012.
Values may be sent and summed in bfloat16 or wider, within the bound.
No kernel may reach another device: no remote copies, remote signals or barrier semaphores. Data moves between devices by JAX's collectives and lax.ppermute only.
A program may use at most 192 MiB of HBM per device.

v0:
```python
import jax
import jax.numpy as jnp
from jax import lax
from jax.sharding import PartitionSpec as P

QUERY_HEADS = 64
KEY_VALUE_HEADS = 8
HEAD_SIZE = 128
BLOCK_TOKENS = 128
NEG_FILL = -1e30


def combined_all(value, axis, join):
    pieces = jax.tree.map(lambda part: lax.all_gather(part, axis), value)
    head = jax.tree.map(lambda part: part[0], pieces)
    tail = jax.tree.map(lambda part: part[1:], pieces)
    subtotal, _ = lax.scan(lambda subtotal, piece: (join(subtotal, piece), None), head, tail)
    return subtotal


def block_partial(query_block, block_ids, blocked_keys, blocked_values):
    present = block_ids >= 0
    chosen = jnp.maximum(block_ids, 0)
    key_rows = blocked_keys[chosen]
    value_rows = blocked_values[chosen]
    scores = jnp.einsum(
        "tgqd,mbgd->tgqmb", query_block, key_rows, preferred_element_type=jnp.float32
    ) * HEAD_SIZE ** (-0.5)
    keep_mask = present[None, None, None, :, None]
    scores = jnp.where(keep_mask, scores, NEG_FILL)
    top_score = jnp.max(scores, axis=(3, 4))
    raised = jnp.where(keep_mask, jnp.exp(scores - top_score[:, :, :, None, None]), 0.0)
    denom_sum = jnp.sum(raised, axis=(3, 4))
    weighted = jnp.einsum(
        "tgqmb,mbgd->tgqd",
        raised.astype(jnp.bfloat16),
        value_rows,
        preferred_element_type=jnp.float32,
    )
    return (top_score, denom_sum, weighted)


def merge_pair(first, second):
    top_first, sum_first, acc_first = first
    top_second, sum_second, acc_second = second
    top_new = jnp.maximum(top_first, top_second)
    scale_first = jnp.exp(top_first - top_new)
    scale_second = jnp.exp(top_second - top_new)
    sum_new = sum_first * scale_first + sum_second * scale_second
    acc_new = acc_first * scale_first[:, :, None] + acc_second * scale_second[:, :, None]
    return (top_new, sum_new, acc_new)


def on_device(text_states, w_query, w_out, visual_keys, visual_values, block_list):
    tok_count = text_states.shape[0]
    group_count = visual_keys.shape[1] // HEAD_SIZE
    queries_per_group = QUERY_HEADS // KEY_VALUE_HEADS
    head_cols = group_count * queries_per_group
    local_terms = jnp.dot(text_states, w_query, preferred_element_type=jnp.float32)
    query_matrix = lax.psum(local_terms, "vis").astype(jnp.bfloat16)
    block_count = tok_count // BLOCK_TOKENS
    blocked_queries = query_matrix.reshape(
        block_count, BLOCK_TOKENS, group_count, queries_per_group, HEAD_SIZE
    )
    blocked_keys = visual_keys.reshape(-1, BLOCK_TOKENS, group_count, HEAD_SIZE)
    blocked_values = visual_values.reshape(-1, BLOCK_TOKENS, group_count, HEAD_SIZE)
    id_rows = block_list[:, 0, :]

    def per_block(packed):
        return block_partial(packed[0], packed[1], blocked_keys, blocked_values)

    top_score, denom_sum, weighted = lax.map(per_block, (blocked_queries, id_rows))
    top_score = top_score.reshape(tok_count, head_cols)
    denom_sum = denom_sum.reshape(tok_count, head_cols)
    weighted = weighted.reshape(tok_count, head_cols, HEAD_SIZE)
    merged_top, sum_all, acc_all = combined_all((top_score, denom_sum, weighted), "vis", merge_pair)
    attended = (
        (acc_all / sum_all[:, :, None])
        .reshape(tok_count, head_cols * HEAD_SIZE)
        .astype(jnp.bfloat16)
    )
    projected = lax.psum_scatter(
        jnp.dot(attended, w_out, preferred_element_type=jnp.float32),
        ("head", "sec"),
        scatter_dimension=0,
        tiled=True,
    )
    return projected.astype(jnp.bfloat16)


def solution(mesh):
    in_specs = (
        P(None, "vis"),
        P("vis", ("head", "sec")),
        P(("head", "sec"), "vis"),
        P("vis", ("head", "sec")),
        P("vis", ("head", "sec")),
        P(None, "vis", None),
    )
    out_specs = P(("head", "sec"), "vis")
    return jax.shard_map(
        on_device, mesh=mesh, in_specs=in_specs, out_specs=out_specs, check_vma=False
    )
```

profile of v0, /device:TPU:1, one launch (start us, length us, event | category | flops | bytes accessed | tf_op | source)
XLA Modules:
  0.0 589.2 jit_solution(97102992759839472)
XLA Ops:
  8.8 131.1 %all-reduce.1 = bf16[256,1024]{1,0:T(8,128)(2,1)S(1)} all-reduce(f32[256,1024]{1,0:T(8,128)S(1)} %fusion.25), channel_id=1, replica_groups=mesh['head'=4,'vis'=32,'sec'=2] {'vis'}, use_global_device_ids=true, to_apply=%region_0.0 | all-reduce | flops 262144 | bytes 1572864 | tf_op jit(solution)/shard_map/psum | solution.py:60
  140.0 60.2 %while.28 = (s32[]{:T(128)}, f32[2,128,1,8]{1,3,2,0:T(8,128)S(1)}, f32[2,128,1,8]{1,3,2,0:T(8,128)S(1)}, f32[2,128,1,8,128]{4,3,1,0,2:T(8,128)}, s32[2,32]{1,0:T...) while((s32[]{:T(128)}, f32[2,128,1,8]{1,3,2,0:T(8,128)S(1)}, ...), condition=%wide.region_4.5_spmd, body=%wide.region_1.4_spmd.sunk | while | flops 2202008576 | bytes 60069356 | solution.py:72
  140.7 2.3 gather_fusion
  143.7 7.0 %bitcast_reduce_fusion.2 = (f32[128,8]{0,1:T(8,128)S(1)}, f32[32,128,128,8]{2,1,3,0:T(8,128)}) fusion(pred[32]{0:T(512)(128)(4,1)S(1)} %compare_bitcast_fusion.2, bf16[1,128,1,8,128]{4,3,1,0,2:T(8,128)(2,1)S(1)} %constant_dynamic-slice_fusion.3, bf16[32,128,128]{2,1,0:T(8,128)(2,1)S(1)} %gather_fusion), kind=kOutput, calls=%fused_computation.11.clone.1 | convolution fusion | flops 1086323712 | bytes 18092064 | tf_op jit(solution)/shard_map/while/body/eval_jaxpr/tgqd,mbgd->tgqmb/dot_general | solution.py:26
  150.7 2.3 gather_fusion.1
  153.1 7.9 %fusion.38 = f32[1,128,1,8,128]{1,4,3,2,0:T(8,128)S(1)} fusion(f32[32,128,128,8]{2,1,3,0:T(8,128)} %get-tuple-element.247, f32[128,8]{0,1:T(8,128)S(1)} %get-tuple-element.248, pred[32]{0:T(512)(128)(4,1)S(1)} %compare_bitcast_fusion.2, bf16[32,128,128]{2,1,0:T(8,128)(2,1)S(1)} %gather_fusion.1), kind=kOutput, calls=%fused_computation.21.clone.1 | convolution fusion | flops 1094713344 | bytes 18354208 | tf_op jit(solution)/shard_map/while/body/eval_jaxpr/tgqmb,mbgd->tgqd/dot_general | solution.py:34
  162.0 8.0 %fusion.37 = f32[128,8]{0,1:T(8,128)S(1)} fusion(f32[32,128,128,8]{2,1,3,0:T(8,128)} %get-tuple-element.247, f32[128,8]{0,1:T(8,128)S(1)} %get-tuple-element.248, pred[32]{0:T(512)(128)(4,1)S(1)} %compare_bitcast_fusion.2), kind=kLoop, calls=%fused_computation.16.clone.1 | loop fusion | flops 20970496 | bytes 16785440 | tf_op jit(solution)/shard_map/while/body/eval_jaxpr/reduce_sum | solution.py:33
  170.8 2.3 gather_fusion
  173.8 7.0 %bitcast_reduce_fusion.2 = (f32[128,8]{0,1:T(8,128)S(1)}, f32[32,128,128,8]{2,1,3,0:T(8,128)}) fusion(pred[32]{0:T(512)(128)(4,1)S(1)} %compare_bitcast_fusion.2, bf16[1,128,1,8,128]{4,3,1,0,2:T(8,128)(2,1)S(1)} %constant_dynamic-slice_fusion.3, bf16[32,128,128]{2,1,0:T(8,128)(2,1)S(1)} %gather_fusion), kind=kOutput, calls=%fused_computation.11.clone.1 | convolution fusion | flops 1086323712 | bytes 18092064 | tf_op jit(solution)/shard_map/while/body/eval_jaxpr/tgqd,mbgd->tgqmb/dot_general | solution.py:26
  180.8 2.3 gather_fusion.1
  183.2 7.9 %fusion.38 = f32[1,128,1,8,128]{1,4,3,2,0:T(8,128)S(1)} fusion(f32[32,128,128,8]{2,1,3,0:T(8,128)} %get-tuple-element.247, f32[128,8]{0,1:T(8,128)S(1)} %get-tuple-element.248, pred[32]{0:T(512)(128)(4,1)S(1)} %compare_bitcast_fusion.2, bf16[32,128,128]{2,1,0:T(8,128)(2,1)S(1)} %gather_fusion.1), kind=kOutput, calls=%fused_computation.21.clone.1 | convolution fusion | flops 1094713344 | bytes 18354208 | tf_op jit(solution)/shard_map/while/body/eval_jaxpr/tgqmb,mbgd->tgqd/dot_general | solution.py:34
  192.1 8.0 %fusion.37 = f32[128,8]{0,1:T(8,128)S(1)} fusion(f32[32,128,128,8]{2,1,3,0:T(8,128)} %get-tuple-element.247, f32[128,8]{0,1:T(8,128)S(1)} %get-tuple-element.248, pred[32]{0:T(512)(128)(4,1)S(1)} %compare_bitcast_fusion.2), kind=kLoop, calls=%fused_computation.16.clone.1 | loop fusion | flops 20970496 | bytes 16785440 | tf_op jit(solution)/shard_map/while/body/eval_jaxpr/reduce_sum | solution.py:33
  200.2 34.1 %all_gather.9 = f32[32,256,8]{1,2,0:T(8,128)S(1)} all-gather(f32[1,256,8]{1,2,0:T(8,128)S(1)} %bitcast.159), channel_id=1, replica_groups=mesh['head'=4,'vis'=32,'sec'=2] {'vis'}, dimensions={0}, use_global_device_ids=true | all-gather | bytes 270336 | tf_op jit(solution)/shard_map/all_gather | solution.py:14
  234.3 43.5 %all_gather.10 = f32[32,256,8]{1,2,0:T(8,128)S(1)} all-gather(f32[1,256,8]{1,2,0:T(8,128)S(1)} %bitcast.160), channel_id=1, replica_groups=mesh['head'=4,'vis'=32,'sec'=2] {'vis'}, dimensions={0}, use_global_device_ids=true | all-gather | bytes 270336 | tf_op jit(solution)/shard_map/all_gather | solution.py:14
  277.9 178.2 %all-gather.2.cloned.1.call-done = f32[32,256,8,128]{3,2,1,0:T(8,128)} async-done(((f32[1,256,8,128]{3,2,1,0:T(8,128)}), f32[32,256,8,128]{3,2,1,0:T(8,128)}) %all-gather.2.cloned.1.call-update) | async-done | bytes 33554448 | tf_op jit(solution)/shard_map/all_gather | solution.py:14
  456.0 22.7 %slice.33 = f32[31,256,8,128]{3,2,1,0:T(8,128)} slice(f32[32,256,8,128]{3,2,1,0:T(8,128)} %all-gather.2.cloned.1.call-done), slice={[1:32], [0:256], [0:8], [0:128]} | slice | bytes 65011712 | tf_op jit(solution)/shard_map/slice | solution.py:16
  480.0 68.2 %while.29 = (s32[]{:T(128)}, f32[256,8]{0,1:T(8,128)S(1)}, f32[256,8]{0,1:T(8,128)S(1)}, f32[256,8,128]{2,1,0:T(8,128)S(1)}, f32[31,256,8]{1,2,0:T(8,128)S(1)}, ...) while((s32[]{:T(128)}, f32[256,8]{0,1:T(8,128)S(1)}, f32[256,8]{0,1:T(8,128)S(1)}, ...), condition=%wide.region_6.7_spmd, body=%wide.region_5.6_spmd.sunk | while | flops 798722 | bytes 3260509 | solution.py:17
  480.3 1.9 fusion.40
  482.5 1.9 fusion.40
  484.7 1.9 fusion.40
  486.9 1.9 fusion.40
  491.3 1.9 fusion.40
  493.5 1.9 fusion.40
  549.8 31.2 %reduce-scatter.2.cloned.1.call-done = f32[32,256]{1,0:T(8,128)} async-done(((f32[256,256]{1,0:T(8,128)}), f32[32,256]{1,0:T(8,128)}) %reduce-scatter.2.cloned.1.call-update) | async-done | bytes 32784 | tf_op jit(solution)/shard_map/reduce_scatter | solution.py:82
  (156 shorter events, 67.2 us)
Async XLA Ops:
  6.5 1.0 copy-start
  6.5 449.5 %all-gather.2.cloned.1.call-start = ((), (), s32[]{:S(2)}) async-start(), calls=%async_computation.1 | async-start | bytes 34603008 | tf_op jit(solution)/shard_map/all_gather | solution.py:14
  200.2 380.8 %reduce-scatter.2.cloned.1.call-start = ((), (), s32[]{:S(2)}) async-start(), calls=%async_computation.2 | async-start | bytes 294912 | tf_op jit(solution)/shard_map/reduce_scatter | solution.py:82
  456.0 126.4 %copy-start.1 = (bf16[256,1024]{1,0:T(8,128)(2,1)S(1)}, bf16[256,1024]{1,0:T(8,128)(2,1)}, u32[]{:S(2)}) copy-start(bf16[256,1024]{1,0:T(8,128)(2,1)} %param.11) | copy-start | bytes 1572868
  478.7 70.1 %copy-start.2 = (bf16[1024,256]{1,0:T(8,128)(2,1)S(1)}, bf16[1024,256]{1,0:T(8,128)(2,1)}, u32[]{:S(2)}) copy-start(bf16[1024,256]{1,0:T(8,128)(2,1)} %param.12) | copy-start | bytes 1572868
Sparse Core Ops, SparseCore 0:
  200.3 255.6 all-gather.1
  549.9 31.0 reduce-scatter.1
where the time goes:
time: 591 us; the launch traced here: 589 us
  blocking collectives  209 us (35%)
  waiting for transfers between devices  209 us (35%)
  other arithmetic  79.7 us (13%)
  local copies, waits for them, and re-layouts  44.6 us (8%)
  matrix products  31.9 us (5%)
  between operations  13.5 us (2%)
    all_gather x1, waiting for transfers between devices, combined_all(): pieces = jax.tree.map(lambda part: lax.all_gather(part, axis), value)  178 us
    psum x1, blocking collectives, on_device(): query_matrix = lax.psum(local_terms, 'vis').astype(jnp.bfloat16)  131 us
    all_gather x2, blocking collectives, combined_all(): pieces = jax.tree.map(lambda part: lax.all_gather(part, axis), value)  77.6 us
    add x31, other arithmetic, merge_pair(): acc_first * scale_first[:, :, None] + acc_second * scale_second[:, :, None]  58.7 us
    reduce_scatter x1, waiting for transfers between devices, on_device(): lax.psum_scatter(jnp.dot(attended, w_out, preferred_element_type=jnp.floa...  31.2 us
    slice x3, local copies, waits for them, and re-layouts, combined_all(): tail = jax.tree.map(lambda part: part[1:], pieces)  22.7 us
    reduce_sum x2, other arithmetic, block_partial(): denom_sum = jnp.sum(raised, axis=(3, 4))  16 us
    dot_general x2, matrix products, block_partial(): jnp.einsum('tgqmb,mbgd->tgqd', raised.astype(jnp.bfloat16), value_rows, p...  15.7 us
  transfers between devices with their start and end apart: 2, of which 2 were waited for; matrix products, arithmetic and copies ran while one was open for 0% of the time, Pallas kernels for 0%

commit v1 on v0

--- a/solution.py
+++ b/solution.py
@@ -1,3 +1,4 @@
+import functools
 import jax
 import jax.numpy as jnp
 from jax import lax
@@ -8,6 +9,13 @@
 HEAD_SIZE = 128
 BLOCK_TOKENS = 128
 NEG_FILL = -1e30
+
+
+def case_map(arr, peer_axis):
+    return jnp.sum(lax.all_gather(arr, peer_axis), axis=0)
+
+
+_edit_gates = functools.partial(case_map, peer_axis="vis")
 
 
 def combined_all(value, axis, join):
@@ -57,7 +65,7 @@
     queries_per_group = QUERY_HEADS // KEY_VALUE_HEADS
     head_cols = group_count * queries_per_group
     local_terms = jnp.dot(text_states, w_query, preferred_element_type=jnp.float32)
-    query_matrix = lax.psum(local_terms, "vis").astype(jnp.bfloat16)
+    query_matrix = _edit_gates(local_terms).astype(jnp.bfloat16)
     block_count = tok_count // BLOCK_TOKENS
     blocked_queries = query_matrix.reshape(
         block_count, BLOCK_TOKENS, group_count, queries_per_group, HEAD_SIZE

time: 591 us -> 683 us (1.16)
  waiting for transfers between devices: 209 us -> 420 us
  blocking collectives: 209 us -> 79.3 us
  other arithmetic: 79.7 us -> 88.9 us
    all_gather x0 -> x1, waiting for transfers between devices: none -> 236 us  [case_map(): return jnp.sum(lax.all_gather(arr, peer_axis), axis=0)]
    psum x1 -> x0, blocking collectives: 131 us -> none  [on_device(): query_matrix = lax.psum(local_terms, 'vis').astype(jnp.bfloat16)]
    all_gather x1, waiting for transfers between devices: 178 us -> 153 us  [combined_all(): pieces = jax.tree.map(lambda part: lax.all_gather(part, axis), value)]
    reduce_sum x0 -> x1, other arithmetic: none -> 11.9 us  [case_map(): return jnp.sum(lax.all_gather(arr, peer_axis), axis=0)]
  transfers between devices with their start and end apart: 2 -> 3, of which waited for: 2 -> 3; matrix products, arithmetic and copies ran while one was open for 0% -> 0% of each run, Pallas kernels for 0% -> 0%
where the time goes in v1:
time: 683 us; the launch traced here: 681 us
  waiting for transfers between devices  420 us (61%)
  other arithmetic  88.9 us (13%)
  blocking collectives  79.3 us (12%)
  local copies, waits for them, and re-layouts  44.6 us (7%)
  matrix products  33 us (5%)
  between operations  13.2 us (2%)
    all_gather x1, waiting for transfers between devices, case_map(): return jnp.sum(lax.all_gather(arr, peer_axis), axis=0)  236 us
    all_gather x1, waiting for transfers between devices, combined_all(): pieces = jax.tree.map(lambda part: lax.all_gather(part, axis), value)  153 us
    all_gather x2, blocking collectives, combined_all(): pieces = jax.tree.map(lambda part: lax.all_gather(part, axis), value)  79.3 us
    add x31, other arithmetic, merge_pair(): acc_first * scale_first[:, :, None] + acc_second * scale_second[:, :, None]  58.7 us
    reduce_scatter x1, waiting for transfers between devices, on_device(): lax.psum_scatter(jnp.dot(attended, w_out, preferred_element_type=jnp.floa...  31.3 us
    slice x3, local copies, waits for them, and re-layouts, combined_all(): tail = jax.tree.map(lambda part: part[1:], pieces)  22.6 us
    reduce_sum x2, other arithmetic, block_partial(): denom_sum = jnp.sum(raised, axis=(3, 4))  16 us
    dot_general x2, matrix products, block_partial(): jnp.einsum('tgqmb,mbgd->tgqd', raised.astype(jnp.bfloat16), value_rows, p...  15.7 us
  transfers between devices with their start and end apart: 3, of which 3 were waited for; matrix products, arithmetic and copies ran while one was open for 0% of the time, Pallas kernels for 0%

profile of v1, /device:TPU:1, one launch (start us, length us, event | category | flops | bytes accessed | tf_op | source)
XLA Modules:
  0.0 680.9 jit_solution(11785829196143805052)
XLA Ops:
  7.6 2.2 fusion.25
  9.9 236.1 %all-gather.6.cloned.1.call-done = f32[8192,1024]{1,0:T(8,128)} async-done(((f32[256,1024]{1,0:T(8,128)}), f32[8192,1024]{1,0:T(8,128)}) %all-gather.6.cloned.1.call-update) | async-done | bytes 33554448 | tf_op jit(solution)/shard_map/all_gather | solution.py:15
  246.0 11.9 %reduce_sum.18 = bf16[256,1024]{1,0:T(8,128)(2,1)S(1)} reduce(f32[32,256,1024]{2,1,0:T(8,128)} %bitcast.152, f32[]{:T(128)} %constant.40.clone.1), dimensions={0}, to_apply=%region_0.0 | reduce | flops 8126464 | bytes 34078724 | tf_op jit(solution)/shard_map/reduce_sum | solution.py:15
  258.0 57.6 %while.28 = (s32[]{:T(128)}, f32[2,128,1,8]{1,3,2,0:T(8,128)S(1)}, f32[2,128,1,8]{1,3,2,0:T(8,128)S(1)}, f32[2,128,1,8,128]{4,3,1,0,2:T(8,128)}, s32[2,32]{1,0:T...) while((s32[]{:T(128)}, f32[2,128,1,8]{1,3,2,0:T(8,128)S(1)}, ...), condition=%wide.region_4.5_spmd, body=%wide.region_1.4_spmd.sunk | while | flops 2202008576 | bytes 60069356 | solution.py:80
  258.1 2.3 gather_fusion
  260.5 7.0 %bitcast_reduce_fusion.2 = (f32[128,8]{0,1:T(8,128)S(1)}, f32[32,128,128,8]{2,1,3,0:T(8,128)}) fusion(pred[32]{0:T(512)(128)(4,1)S(1)} %compare_bitcast_fusion.2, bf16[1,128,1,8,128]{4,3,1,0,2:T(8,128)(2,1)S(1)} %constant_dynamic-slice_fusion.3, bf16[32,128,128]{2,1,0:T(8,128)(2,1)S(1)} %gather_fusion), kind=kOutput, calls=%fused_computation.11.clone.1 | convolution fusion | flops 1086323712 | bytes 18092064 | tf_op jit(solution)/shard_map/while/body/eval_jaxpr/tgqd,mbgd->tgqmb/dot_general | solution.py:34
  267.5 2.3 gather_fusion.1
  269.8 7.9 %fusion.38 = f32[1,128,1,8,128]{1,4,3,2,0:T(8,128)S(1)} fusion(f32[32,128,128,8]{2,1,3,0:T(8,128)} %get-tuple-element.239, f32[128,8]{0,1:T(8,128)S(1)} %get-tuple-element.240, pred[32]{0:T(512)(128)(4,1)S(1)} %compare_bitcast_fusion.2, bf16[32,128,128]{2,1,0:T(8,128)(2,1)S(1)} %gather_fusion.1), kind=kOutput, calls=%fused_computation.21.clone.1 | convolution fusion | flops 1094713344 | bytes 18354208 | tf_op jit(solution)/shard_map/while/body/eval_jaxpr/tgqmb,mbgd->tgqd/dot_general | solution.py:42
  278.8 8.0 %fusion.37 = f32[128,8]{0,1:T(8,128)S(1)} fusion(f32[32,128,128,8]{2,1,3,0:T(8,128)} %get-tuple-element.239, f32[128,8]{0,1:T(8,128)S(1)} %get-tuple-element.240, pred[32]{0:T(512)(128)(4,1)S(1)} %compare_bitcast_fusion.2), kind=kLoop, calls=%fused_computation.16.clone.1 | loop fusion | flops 20970496 | bytes 16785440 | tf_op jit(solution)/shard_map/while/body/eval_jaxpr/reduce_sum | solution.py:41
  286.8 2.3 gather_fusion
  289.2 7.0 %bitcast_reduce_fusion.2 = (f32[128,8]{0,1:T(8,128)S(1)}, f32[32,128,128,8]{2,1,3,0:T(8,128)}) fusion(pred[32]{0:T(512)(128)(4,1)S(1)} %compare_bitcast_fusion.2, bf16[1,128,1,8,128]{4,3,1,0,2:T(8,128)(2,1)S(1)} %constant_dynamic-slice_fusion.3, bf16[32,128,128]{2,1,0:T(8,128)(2,1)S(1)} %gather_fusion), kind=kOutput, calls=%fused_computation.11.clone.1 | convolution fusion | flops 1086323712 | bytes 18092064 | tf_op jit(solution)/shard_map/while/body/eval_jaxpr/tgqd,mbgd->tgqmb/dot_general | solution.py:34
  296.2 2.3 gather_fusion.1
  298.6 7.9 %fusion.38 = f32[1,128,1,8,128]{1,4,3,2,0:T(8,128)S(1)} fusion(f32[32,128,128,8]{2,1,3,0:T(8,128)} %get-tuple-element.239, f32[128,8]{0,1:T(8,128)S(1)} %get-tuple-element.240, pred[32]{0:T(512)(128)(4,1)S(1)} %compare_bitcast_fusion.2, bf16[32,128,128]{2,1,0:T(8,128)(2,1)S(1)} %gather_fusion.1), kind=kOutput, calls=%fused_computation.21.clone.1 | convolution fusion | flops 1094713344 | bytes 18354208 | tf_op jit(solution)/shard_map/while/body/eval_jaxpr/tgqmb,mbgd->tgqd/dot_general | solution.py:42
  307.6 8.0 %fusion.37 = f32[128,8]{0,1:T(8,128)S(1)} fusion(f32[32,128,128,8]{2,1,3,0:T(8,128)} %get-tuple-element.239, f32[128,8]{0,1:T(8,128)S(1)} %get-tuple-element.240, pred[32]{0:T(512)(128)(4,1)S(1)} %compare_bitcast_fusion.2), kind=kLoop, calls=%fused_computation.16.clone.1 | loop fusion | flops 20970496 | bytes 16785440 | tf_op jit(solution)/shard_map/while/body/eval_jaxpr/reduce_sum | solution.py:41
  315.7 39.5 %all_gather.17 = f32[32,256,8]{1,2,0:T(8,128)S(1)} all-gather(f32[1,256,8]{1,2,0:T(8,128)S(1)} %bitcast.161), channel_id=1, replica_groups=mesh['head'=4,'vis'=32,'sec'=2] {'vis'}, dimensions={0}, use_global_device_ids=true | all-gather | bytes 270336 | tf_op jit(solution)/shard_map/all_gather | solution.py:22
  355.2 39.8 %all_gather.18 = f32[32,256,8]{1,2,0:T(8,128)S(1)} all-gather(f32[1,256,8]{1,2,0:T(8,128)S(1)} %bitcast.162), channel_id=1, replica_groups=mesh['head'=4,'vis'=32,'sec'=2] {'vis'}, dimensions={0}, use_global_device_ids=true | all-gather | bytes 270336 | tf_op jit(solution)/shard_map/all_gather | solution.py:22
  395.0 152.9 %all-gather.4.cloned.1.call-done = f32[32,256,8,128]{3,2,1,0:T(8,128)} async-done(((f32[1,256,8,128]{3,2,1,0:T(8,128)}), f32[32,256,8,128]{3,2,1,0:T(8,128)}) %all-gather.4.cloned.1.call-update) | async-done | bytes 33554448 | tf_op jit(solution)/shard_map/all_gather | solution.py:22
  547.9 22.6 %slice.33 = f32[31,256,8,128]{3,2,1,0:T(8,128)} slice(f32[32,256,8,128]{3,2,1,0:T(8,128)} %all-gather.4.cloned.1.call-done), slice={[1:32], [0:256], [0:8], [0:128]} | slice | bytes 65011712 | tf_op jit(solution)/shard_map/slice | solution.py:24
  571.9 68.2 %while.29 = (s32[]{:T(128)}, f32[256,8]{0,1:T(8,128)S(1)}, f32[256,8]{0,1:T(8,128)S(1)}, f32[256,8,128]{2,1,0:T(8,128)S(1)}, f32[31,256,8]{1,2,0:T(8,128)S(1)}, ...) while((s32[]{:T(128)}, f32[256,8]{0,1:T(8,128)S(1)}, f32[256,8]{0,1:T(8,128)S(1)}, ...), condition=%wide.region_6.7_spmd, body=%wide.region_5.6_spmd.sunk | while | flops 798722 | bytes 3260509 | solution.py:25
  572.2 1.9 fusion.40
  576.6 1.9 fusion.40
  578.8 1.9 fusion.40
  581.0 1.9 fusion.40
  641.7 31.3 %reduce-scatter.2.cloned.1.call-done = f32[32,256]{1,0:T(8,128)} async-done(((f32[256,256]{1,0:T(8,128)}), f32[32,256]{1,0:T(8,128)}) %reduce-scatter.2.cloned.1.call-update) | async-done | bytes 32784 | tf_op jit(solution)/shard_map/reduce_scatter | solution.py:90
  (161 shorter events, 67.2 us)
Async XLA Ops:
  6.5 1.0 copy-start
  6.5 239.5 %all-gather.6.cloned.1.call-start = ((), (), s32[]{:S(2)}) async-start(), calls=%async_computation.3 | async-start | bytes 34603008 | tf_op jit(solution)/shard_map/all_gather | solution.py:15
  9.8 538.1 %all-gather.4.cloned.1.call-start = ((), (), s32[]{:S(2)}) async-start(), calls=%async_computation.1 | async-start | bytes 34603008 | tf_op jit(solution)/shard_map/all_gather | solution.py:22
  246.0 12.0 %copy-start.3 = (s32[2,1,32]{2,1,0:T(1,128)S(1)}, s32[2,1,32]{2,1,0:T(1,128)}, u32[]{:S(2)}) copy-start(s32[2,1,32]{2,1,0:T(1,128)} %param.15) | copy-start | bytes 772
  315.6 357.4 %reduce-scatter.2.cloned.1.call-start = ((), (), s32[]{:S(2)}) async-start(), calls=%async_computation.2 | async-start | bytes 294912 | tf_op jit(solution)/shard_map/reduce_scatter | solution.py:90
  547.9 126.4 %copy-start.1 = (bf16[256,1024]{1,0:T(8,128)(2,1)S(1)}, bf16[256,1024]{1,0:T(8,128)(2,1)}, u32[]{:S(2)}) copy-start(bf16[256,1024]{1,0:T(8,128)(2,1)} %param.11) | copy-start | bytes 1572868
  570.5 70.1 %copy-start.2 = (bf16[1024,256]{1,0:T(8,128)(2,1)S(1)}, bf16[1024,256]{1,0:T(8,128)(2,1)}, u32[]{:S(2)}) copy-start(bf16[1024,256]{1,0:T(8,128)(2,1)} %param.12) | copy-start | bytes 1572868
Sparse Core Ops, SparseCore 0:
  10.0 235.9 all-gather.5
  315.7 232.1 all-gather.3
  641.8 31.1 reduce-scatter.1
